TPU v7x, 128 devices: a whole 4x4x4 slice. The times are simulated.
128 devices in a mesh: tm: 4 (over x_hi, core), space: 32 (over x_lo, z, y).
Axes of the slice: x: 4 (x_hi: 2, x_lo: 2; x = x_hi * 2 + x_lo), y: 4, z: 4, core: 2. Of those that a mesh axis runs over, the one named last changes fastest.
Arguments:
- queries: bfloat16 [4, 32, 2, 256, 1536], P('tm', 'space'), may hold values from -8 to 8
- keys: bfloat16 [4, 32, 2, 256, 1536], P('tm', 'space'), may hold values from -6 to 6
- values: bfloat16 [4, 32, 2, 256, 1536], P('tm', 'space'), may hold values from -6 to 6
- tile_mask: int32 [4, 32, 2, 27], P('tm', 'space'), may hold values 0 or 1
- head_reach: int32 [12, 3], replicated, may hold values from 0 to 1, as said below
Outputs:
- attended: bfloat16 [4, 32, 2, 256, 1536], P('tm', 'space')
Inputs may be any that keep to these rules, and one draw needn't show every extreme that they name: `head_reach`: some head has reach 1 along all three dimensions.
All inputs are finite; a program needn't handle non-finite values. No bound on the sum of `tile_mask` on one device may be relied on, other than what follows from the above.
Results may differ from a plain program's by a relative error of at most 0.0034.
Values may be sent and summed in bfloat16 or wider, within the bound.
No kernel may reach another device: no remote copies, remote signals or barrier semaphores. Data moves between devices by JAX's collectives and lax.ppermute only.
A program may use at most 320 MiB of HBM per device.

v0:
```python
import jax
import jax.numpy as jnp
from jax import lax
from jax.sharding import PartitionSpec as P

HD = 128


def extended_2(block, sides, width):
    for axis, dim in sides:
        count = lax.axis_size(axis)
        forward = [(i, i + 1) for i in range(count - 1)]
        backward = [(target, source) for source, target in forward]
        low = lax.ppermute(
            lax.slice_in_dim(block, block.shape[dim] - width, None, axis=dim), axis, forward
        )
        high = lax.ppermute(lax.slice_in_dim(block, 0, width, axis=dim), axis, backward)
        block = jnp.concatenate([low, block, high], axis=dim)
    return block


def passed_along(value, axis, by):
    count = lax.axis_size(axis)
    pairs = [(i, i + by) for i in range(count) if 0 <= i + by < count]
    return lax.ppermute(value, axis, pairs)


def tile_allow(
    mask_row, reach, frame_pos, height_pos, width_pos, frame_count, height_count, width_count
):
    shift = jnp.arange(3, dtype=jnp.int32) - 1
    frame_step = shift[:, None, None]
    height_step = shift[None, :, None]
    width_step = shift[None, None, :]
    inside = (frame_pos + frame_step >= 0) & (frame_pos + frame_step < frame_count)
    inside = inside & (height_pos + height_step >= 0) & (height_pos + height_step < height_count)
    inside = inside & (width_pos + width_step >= 0) & (width_pos + width_step < width_count)
    picked = mask_row.reshape(3, 3, 3)
    center = (frame_step == 0) & (height_step == 0) & (width_step == 0)
    tile_ok = inside & ((picked == 1) | center)
    within = jnp.abs(frame_step)[None] <= reach[:, 0, None, None, None]
    within = within & (jnp.abs(height_step)[None] <= reach[:, 1, None, None, None])
    within = within & (jnp.abs(width_step)[None] <= reach[:, 2, None, None, None])
    return tile_ok[None] & within


def attend(query_tile, key_rows, value_rows, allow):
    heads = allow.shape[0]
    tile_len = query_tile.shape[0]
    token_allow = jnp.repeat(allow.reshape(heads, -1), tile_len, axis=1)

    def per_head(head):
        query_head = lax.dynamic_slice_in_dim(query_tile, head * HD, HD, 1)
        key_head = lax.dynamic_slice_in_dim(key_rows, head * HD, HD, 1)
        value_head = lax.dynamic_slice_in_dim(value_rows, head * HD, HD, 1)
        usable = token_allow[head]
        scores = lax.dot_general(
            query_head, key_head, (((1,), (1,)), ((), ())), preferred_element_type=jnp.float32
        ) * HD ** (-0.5)
        scores = jnp.where(usable[None, :], scores, jnp.float32(-1e30))
        largest = jnp.max(scores, axis=1, keepdims=True)
        weights = jnp.where(usable[None, :], jnp.exp(scores - largest), jnp.float32(0.0))
        totals = jnp.sum(weights, axis=1, keepdims=True)
        rounded = weights.astype(jnp.bfloat16)
        return jnp.dot(rounded, value_head, preferred_element_type=jnp.float32) / totals

    result = lax.map(per_head, jnp.arange(heads, dtype=jnp.int32))
    return jnp.transpose(result, (1, 0, 2)).reshape(tile_len, heads * HD).astype(jnp.bfloat16)


def frame_step_in(block):
    return extended_2(block, (("tm", 1),), 1)


def plane_step_in(block):
    above = passed_along(block, "space", 1)
    below = passed_along(block, "space", -1)
    return jnp.concatenate([above, block, below], axis=2)


def local(queries, keys, values, tile_mask, head_reach):
    width_count = queries.shape[2]
    tile_len = queries.shape[3]
    width = queries.shape[4]
    key_value = jnp.stack([keys, values])
    extended = plane_step_in(frame_step_in(key_value))
    padded = jnp.pad(extended, ((0, 0), (0, 0), (0, 0), (1, 1), (0, 0), (0, 0)))
    frame_pos = lax.axis_index("tm")
    height_pos = lax.axis_index("space")
    frame_count = lax.axis_size("tm")
    height_count = lax.axis_size("space")
    outputs = []
    for column in range(width_count):
        key_rows = padded[0, :, :, column : column + 3].reshape(-1, width)
        value_rows = padded[1, :, :, column : column + 3].reshape(-1, width)
        allow = tile_allow(
            tile_mask[0, 0, column],
            head_reach,
            frame_pos,
            height_pos,
            column,
            frame_count,
            height_count,
            width_count,
        )
        outputs.append(attend(queries[0, 0, column], key_rows, value_rows, allow))
    return jnp.stack(outputs).reshape(1, 1, width_count, tile_len, width)


def solution(mesh):
    in_specs = (
        P("tm", "space", None, None, None),
        P("tm", "space", None, None, None),
        P("tm", "space", None, None, None),
        P("tm", "space", None, None),
        P(),
    )
    out_specs = P("tm", "space", None, None, None)
    return jax.shard_map(local, mesh=mesh, in_specs=in_specs, out_specs=out_specs, check_vma=False)
```

profile of v0, /device:TPU:6, one launch (start us, length us, event | category | flops | bytes accessed | tf_op | source)
XLA Modules:
  0.0 584.9 jit_solution(11188421790367140380)
XLA Ops:
  4.3 5.1 collective-permute-start.1
  9.4 43.0 %collective-permute-done = bf16[2,1,1,2,256,1536]{5,4,3,2,1,0:T(8,128)(2,1)S(1)} collective-permute-done((bf16[2,1,1,2,256,1536]{5,4,3,2,1,0:T(8,128)(2,1)S(1)}, bf16[2,1,1,2,256,1536]{5,4,3,2,1,0:T(8,128)(2,1)S(1)}, u32[]{:S(2)}, u32[]{:S(2)}) %collective-permute-start) | collective-permute-done | bytes 3145760 | tf_op jit(solution)/shard_map/ppermute | solution.py:14
  52.5 8.5 %collective-permute-done.1 = bf16[2,1,1,2,256,1536]{5,4,3,2,1,0:T(8,128)(2,1)S(1)} collective-permute-done((bf16[2,1,1,2,256,1536]{5,4,3,2,1,0:T(8,128)(2,1)S(1)}, bf16[2,1,1,2,256,1536]{5,4,3,2,1,0:T(8,128)(2,1)S(1)}, u32[]{:S(2)}, u32[]{:S(2)}) %collective-permute-start.1) | collective-permute-done | bytes 3145760 | tf_op jit(solution)/shard_map/ppermute | solution.py:17
  61.0 4.5 pad_maximum_fusion
  67.5 17.1 %collective-permute-start.3 = (bf16[2,3,1,2,256,1536]{5,4,3,2,1,0:T(8,128)(2,1)}, bf16[2,3,1,2,256,1536]{5,4,3,2,1,0:T(8,128)(2,1)}, u32[]{:S(2)}, u32[]{:S(2)}) collective-permute-start(bf16[2,3,1,2,256,1536]{5,4,3,2,1,0:T(8,128)(2,1)} %pad_maximum_fusion), channel_id=1, source_target_pairs={{1,0},{2,1},{3,2},{4,3},{5,4},{6,5},{7,6},{8,7},{9,8},{10,9},{11,1... | collective-permute-start | bytes 28311560 | tf_op jit(solution)/shard_map/ppermute | solution.py:25
  88.8 165.0 %collective-permute-done.2 = bf16[2,3,1,2,256,1536]{5,4,3,2,1,0:T(8,128)(2,1)} collective-permute-done((bf16[2,3,1,2,256,1536]{5,4,3,2,1,0:T(8,128)(2,1)}, bf16[2,3,1,2,256,1536]{5,4,3,2,1,0:T(8,128)(2,1)}, u32[]{:S(2)}, u32[]{:S(2)}) %collective-permute-start.2) | collective-permute-done | bytes 9437216 | tf_op jit(solution)/shard_map/ppermute | solution.py:25
  253.8 26.3 %select_maximum_fusion = bf16[2,3,3,4,256,1536]{5,4,3,2,1,0:T(8,128)(2,1)} fusion(bf16[2,3,1,2,256,1536]{5,4,3,2,1,0:T(8,128)(2,1)} %collective-permute-done.3, bf16[2,3,1,2,256,1536]{5,4,3,2,1,0:T(8,128)(2,1)} %collective-permute-done.2, bf16[2,1,1,2,256,1536]{5,4,3,2,1,0:T(8,128)(2,1)} %copy-done.3, bf16[2,1,1,2,256,1536]{5,4,3,2,1,0:T(8,128)(2,1)} %copy-done.2, ...), kind=kLoop, calls=%fused_computation.41 | loop fusion | flops 594542592 | bytes 84934656 | tf_op jit(solution)/shard_map/concatenate | solution.py:78
  280.0 53.6 %fusion.67 = (bf16[1,3,3,3,256,1536]{5,4,3,2,1,0:T(8,128)(2,1)}, bf16[1,3,3,3,256,1536]{5,4,3,2,1,0:T(8,128)(2,1)}, bf16[1,3,3,3,256,1536]{5,4,3,2,1,0:T(8,128)(2,1)}, bf16[1,3,3,3,256,1536]{5,4,3,2,1,0:T(8,128)(2,1)}) fusion(bf16[2,3,3,4,256,1536]{5,4,3,2,1,0:T(8,128)(2,1)} %select_maximum_fusion), kind=kLoop, calls=%fused_computation.86 | loop fusion | bytes 169869312 | tf_op jit(solution)/shard_map/slice | solution.py:95
  333.7 122.6 %while.20 = (s32[]{:T(128)}, bf16[12,256,128]{1,2,0:T(8,128)(2,1)S(1)}, s32[12]{0:T(128)S(1)}, pred[12,6912]{1,0:T(8,128)(4,1)S(1)}, bf16[256,1536]{1,0:T(8,128)...) while((s32[]{:T(128)}, ...), condition=%wide.region_3.4_spmd, body=%wide.region_0.3_spmd.sunk | while | flops 921959936 | bytes 25206748 | solution.py:67
  336.6 2.8 fusion.80
  340.9 2.8 fusion.82
  346.9 2.8 fusion.80
  351.1 2.8 fusion.82
  361.4 2.8 fusion.82
  371.6 2.8 fusion.82
  381.8 2.8 fusion.82
  392.0 2.8 fusion.82
  397.9 2.8 fusion.80
  402.2 2.8 fusion.82
  408.1 2.8 fusion.80
  412.4 2.8 fusion.82
  422.6 2.8 fusion.82
  432.9 2.8 fusion.82
  443.1 2.8 fusion.82
  453.3 2.8 fusion.82
  456.4 126.8 %while.21 = (s32[]{:T(128)}, bf16[12,256,128]{1,2,0:T(8,128)(2,1)S(1)}, s32[12]{0:T(128)S(1)}, pred[12,6912]{1,0:T(8,128)(4,1)S(1)}, bf16[256,1536]{1,0:T(8,128)...) while((s32[]{:T(128)}, ...), condition=%wide.region_7.8_spmd, body=%wide.region_4.7_spmd.sunk | while | flops 921959936 | bytes 25206748 | solution.py:67
  459.7 2.8 fusion.85
  464.0 2.8 fusion.87
  474.5 2.8 fusion.87
  480.8 2.8 fusion.85
  485.1 2.8 fusion.87
  491.4 2.8 fusion.85
  495.7 2.8 fusion.87
  501.9 2.8 fusion.85
  506.2 2.8 fusion.87
  512.5 2.8 fusion.85
  516.8 2.8 fusion.87
  523.1 2.8 fusion.85
  527.4 2.8 fusion.87
  533.6 2.8 fusion.85
  537.9 2.8 fusion.87
  544.2 2.8 fusion.85
  548.5 2.8 fusion.87
  554.8 2.8 fusion.85
  559.1 2.8 fusion.87
  569.7 2.8 fusion.87
  575.9 2.8 fusion.85
  580.2 2.8 fusion.87
  (181 shorter events, 95.6 us)
Async XLA Ops:
  0.0 61.0 %copy-start = (bf16[1,1,2,256,1536]{4,3,2,1,0:T(8,128)(2,1)S(1)}, bf16[1,1,2,256,1536]{4,3,2,1,0:T(8,128)(2,1)}, u32[]{:S(2)}) copy-start(bf16[1,1,2,256,1536]{4,3,2,1,0:T(8,128)(2,1)} %param.11) | copy-start | bytes 4718596
  0.0 61.0 %copy-start.1 = (bf16[1,1,2,256,1536]{4,3,2,1,0:T(8,128)(2,1)S(1)}, bf16[1,1,2,256,1536]{4,3,2,1,0:T(8,128)(2,1)}, u32[]{:S(2)}) copy-start(bf16[1,1,2,256,1536]{4,3,2,1,0:T(8,128)(2,1)} %param.10) | copy-start | bytes 4718596
  2.3 82.2 %copy-start.4 = (s32[12,3]{0,1:T(4,128)S(1)}, s32[12,3]{0,1:T(4,128)}, u32[]{:S(2)}) copy-start(s32[12,3]{0,1:T(4,128)} %param.13) | copy-start | bytes 436
  2.3 83.0 %copy-start.5 = (s32[1,1,2,27]{3,2,1,0:T(2,128)S(1)}, s32[1,1,2,27]{3,2,1,0:T(2,128)}, u32[]{:S(2)}) copy-start(s32[1,1,2,27]{3,2,1,0:T(2,128)} %param.12) | copy-start | bytes 652
  2.4 50.1 %collective-permute-start = (bf16[2,1,1,2,256,1536]{5,4,3,2,1,0:T(8,128)(2,1)S(1)}, bf16[2,1,1,2,256,1536]{5,4,3,2,1,0:T(8,128)(2,1)S(1)}, u32[]{:S(2)}, u32[]{:S(2)}) collective-permute-start(bf16[2,1,1,2,256,1536]{5,4,3,2,1,0:T(8,128)(2,1)S(1)} %pad_maximum_fusion.1), channel_id=1, source_target_pairs={{0,32},{32,64},{64,96},{1,33},{33,65},{65,97},{2,34},{34,66},{66,9... | collective-permute-start | bytes 9437192 | tf_op jit(solution)/shard_map/ppermute | solution.py:14
  4.3 56.7 %collective-permute-start.1 = (bf16[2,1,1,2,256,1536]{5,4,3,2,1,0:T(8,128)(2,1)S(1)}, bf16[2,1,1,2,256,1536]{5,4,3,2,1,0:T(8,128)(2,1)S(1)}, u32[]{:S(2)}, u32[]{:S(2)}) collective-permute-start(bf16[2,1,1,2,256,1536]{5,4,3,2,1,0:T(8,128)(2,1)S(1)} %pad_maximum_fusion.1), channel_id=1, source_target_pairs={{32,0},{64,32},{96,64},{33,1},{65,33},{97,65},{34,2},{66,34},{98,6... | collective-permute-start | bytes 9437192 | tf_op jit(solution)/shard_map/ppermute | solution.py:17
  52.5 13.0 %copy-start.2 = (bf16[2,1,1,2,256,1536]{5,4,3,2,1,0:T(8,128)(2,1)}, bf16[2,1,1,2,256,1536]{5,4,3,2,1,0:T(8,128)(2,1)S(1)}, u32[]{:S(2)}) copy-start(bf16[2,1,1,2,256,1536]{5,4,3,2,1,0:T(8,128)(2,1)S(1)} %collective-permute-done) | copy-start | bytes 9437188
  61.0 4.5 copy-start.3
  65.5 188.2 %collective-permute-start.2 = (bf16[2,3,1,2,256,1536]{5,4,3,2,1,0:T(8,128)(2,1)}, bf16[2,3,1,2,256,1536]{5,4,3,2,1,0:T(8,128)(2,1)}, u32[]{:S(2)}, u32[]{:S(2)}) collective-permute-start(bf16[2,3,1,2,256,1536]{5,4,3,2,1,0:T(8,128)(2,1)} %pad_maximum_fusion), channel_id=1, source_target_pairs={{0,1},{1,2},{2,3},{3,4},{4,5},{5,6},{6,7},{7,8},{8,9},{9,10},{10,1... | collective-permute-start | bytes 28311560 | tf_op jit(solution)/shard_map/ppermute | solution.py:25
  67.5 186.3 %collective-permute-start.3 = (bf16[2,3,1,2,256,1536]{5,4,3,2,1,0:T(8,128)(2,1)}, bf16[2,3,1,2,256,1536]{5,4,3,2,1,0:T(8,128)(2,1)}, u32[]{:S(2)}, u32[]{:S(2)}) collective-permute-start(bf16[2,3,1,2,256,1536]{5,4,3,2,1,0:T(8,128)(2,1)} %pad_maximum_fusion), channel_id=1, source_target_pairs={{1,0},{2,1},{3,2},{4,3},{5,4},{6,5},{7,6},{8,7},{9,8},{10,9},{11,1... | collective-permute-start | bytes 28311560 | tf_op jit(solution)/shard_map/ppermute | solution.py:25
where the time goes:
time: 587 us; the launch traced here: 585 us
  waiting for transfers between devices  217 us (37%)
  matrix products  135 us (23%)
  local copies, waits for them, and re-layouts  78.2 us (13%)
  other arithmetic  70.2 us (12%)
  loops' own time  59 us (10%)
  starting transfers between devices  26 us (4%)
    ppermute x2, waiting for transfers between devices, passed_along(): return lax.ppermute(value, axis, pairs)  165 us
    dot_general x24, matrix products, per_head(): jnp.dot(rounded, value_head, preferred_element_type=jnp.float32) / totals  68.1 us
    dot_general x24, matrix products, per_head(): lax.dot_general(query_head, key_head, (((1,), (1,)), ((), ())), preferred...  66.6 us
    another operation x2, loops' own time, attend(): result = lax.map(per_head, jnp.arange(heads, dtype=jnp.int32))  59 us
    slice x1, local copies, waits for them, and re-layouts, local(): value_rows = padded[1, :, :, column:column + 3].reshape(-1, width)  53.6 us
    ppermute x1, waiting for transfers between devices, extended_2(): lax.ppermute(lax.slice_in_dim(block, block.shape[dim] - width, None, axis...  43 us
    reduce_sum x24, other arithmetic, per_head(): totals = jnp.sum(weights, axis=1, keepdims=True)  36.5 us
    concatenate x1, other arithmetic, plane_step_in(): return jnp.concatenate([above, block, below], axis=2)  26.3 us
  transfers between devices with their start and end apart: 4, of which 3 were waited for; matrix products, arithmetic and copies ran while one was open for 1% of the time, Pallas kernels for 0%

commit v1 on v0

v1 whole, which is shorter than its diff:
```python
import functools
import math

import jax
import jax.numpy as jnp
from jax import lax
from jax.experimental import pallas as pl
from jax.experimental.pallas import tpu as pltpu
from jax.sharding import PartitionSpec as P

HD = 128
SCALE = HD ** (-0.5) * math.log2(math.e)
LOW = -1e30
BF = jnp.bfloat16
F32 = jnp.float32
ANY = pl.BlockSpec(memory_space=pl.ANY)
SMEM = pl.BlockSpec(memory_space=pltpu.SMEM)

BRANCHES = ((12, 12, 12),)

T_HORD, T_FORD, T_HSLOT, T_FSLOT, T_NH, T_NF, T_NC, T_FRAME, T_HEIGHT, T_PICK = (
    0, 16, 32, 48, 64, 65, 66, 67, 68, 69,
)
T_LEN = 80


def shift(value, axis, by):
    count = lax.axis_size(axis)
    return lax.ppermute(value, axis, [(i, i + by) for i in range(count) if 0 <= i + by < count])


def meta_kernel(heads, branches, reach, table):
    def count(member):
        total = jnp.int32(0)
        for h in range(heads):
            total = total + member(h).astype(jnp.int32)
        return total

    def fill(base, slots, groups):
        filled = jnp.int32(0)
        for member in groups:
            for h in range(heads):
                hit = member(h)
                table[jnp.where(hit, base + filled, base + 15)] = jnp.int32(h)
                table[jnp.where(hit, slots + h, slots + 15)] = filled
                filled = filled + hit.astype(jnp.int32)

    frames = lambda h: reach[h, 0] > 0
    heights = lambda h: reach[h, 1] > 0
    corner = lambda h: frames(h) & heights(h)
    fill(T_HORD, T_HSLOT, (corner, lambda h: heights(h) & ~frames(h), lambda h: ~heights(h)))
    fill(T_FORD, T_FSLOT, (corner, lambda h: frames(h) & ~heights(h), lambda h: ~frames(h)))
    nh, nf, nc = count(heights), count(frames), count(corner)
    table[T_NH] = nh
    table[T_NF] = nf
    table[T_NC] = nc
    table[T_FRAME] = lax.axis_index("tm").astype(jnp.int32)
    table[T_HEIGHT] = lax.axis_index("space").astype(jnp.int32)
    pick = jnp.int32(len(branches) - 1)
    for i in reversed(range(len(branches))):
        most_h, most_c, most_f = branches[i]
        fits = (nh <= most_h) & (nc <= most_c) & (nf <= most_f)
        pick = jnp.where(fits, jnp.int32(i), pick)
    table[T_PICK] = pick


def pack_kernel(sizes, table, keys, values, *rest):
    outs, (buf, in_sem, out_sem) = rest[: len(sizes)], rest[len(sizes) :]
    slots = []
    for out, (base, start, size) in zip(outs, sizes):
        slots += [(out, i, base + start + i) for i in range(size)]
    reads = []
    for s, (_, _, where) in enumerate(slots):
        lanes = pl.ds(pl.multiple_of(table[where] * HD, HD), HD)
        pair = [
            pltpu.make_async_copy(a.at[:, :, lanes], buf.at[s, j], in_sem.at[s, j])
            for j, a in enumerate((keys, values))
        ]
        for copy in pair:
            copy.start()
        reads.append(pair)
    writes = []
    for s, (out, i, _) in enumerate(slots):
        for copy in reads[s]:
            copy.wait()
        copy = pltpu.make_async_copy(buf.at[s], out.at[i], out_sem.at[s])
        copy.start()
        writes.append(copy)
    for copy in writes:
        copy.wait()


def scores_of(query, key):
    return lax.dot_general(query, key, (((1,), (1,)), ((), ())), preferred_element_type=F32)


def step(query, tiles, state):
    scores = [scores_of(query, key) for key, _, _ in tiles]
    tops = []
    for s, (_, _, valid) in zip(scores, tiles):
        top = jnp.max(s, axis=1, keepdims=True) * F32(SCALE)
        tops.append(top if valid is None else jnp.where(valid, top, F32(LOW)))
    largest = functools.reduce(jnp.maximum, tops)
    if state is not None:
        old, old_sum, old_acc = state
        largest = jnp.maximum(largest, old)
    total, acc = None, None
    for s, (_, value, valid) in zip(scores, tiles):
        base = largest if valid is None else jnp.where(valid, largest, F32(-LOW))
        weights = jnp.exp2(s * F32(SCALE) - base)
        part = jnp.sum(weights, axis=1, keepdims=True)
        out = jnp.dot(weights.astype(BF), value, preferred_element_type=F32)
        total = part if total is None else total + part
        acc = out if acc is None else acc + out
    if state is not None:
        fade = jnp.exp2(old - largest)
        total = total + fade * old_sum
        acc = acc + fade * old_acc
    return largest, total, acc


def put_stats(ref, where, largest, total):
    lane = lax.broadcasted_iota(jnp.int32, (largest.shape[0], HD), 1)
    ref[where] = jnp.where(lane < HD // 2, largest, total)


def get_stats(stats):
    return stats[:, 0:1], stats[:, HD // 2 : HD // 2 + 1]


def own_kernel(reach, mask, query, key, value, acc_out, stat_out):
    head = pl.program_id(0)
    for c in range(2):
        side = (reach[head, 2] > 0) & (mask[c, 13 + 1 - 2 * c] == 1)
        q = query[c]
        tiles = [(key[c], value[c], None), (key[1 - c], value[1 - c], side)]
        largest, total, acc = step(q, tiles, None)
        acc_out[0, c] = acc
        put_stats(stat_out, (0, c), largest, total)


def far_kernel(spec, last, table, reach, mask, *rest):
    n_bufs = sum(len(s[3]) for s in spec)
    bufs = rest[:n_bufs]
    rest = rest[n_bufs:]
    if last:
        _, query, acc_in, stat_in, out = rest[:5]
        rest = rest[5:]
    else:
        query, acc_in, stat_in, out, acc_out, stat_out = rest[:6]
        rest = rest[6:]
    held, sem, acc_s, max_s, sum_s, lists = rest
    i = pl.program_id(0)
    head = table[T_HORD + i]
    copies = []
    base = 0
    for frame, height, kind, pieces in spec:
        count = table[{"h": T_NH, "f": T_NF, "c": T_NC}[kind]]
        size = 0
        for ref, start, length in pieces:
            for j in range(length):
                slot = base + start + j
                copies.append(
                    (pltpu.make_async_copy(bufs[ref].at[j], held.at[slot], sem.at[slot]), start + j < count)
                )
            size += length
        base += size

    @pl.when(i == 0)
    def _():
        for copy, wanted in copies:
            pl.when(wanted)(copy.start)

    counts = [jnp.int32(0), jnp.int32(0)]
    base = 0
    for frame, height, kind, pieces in spec:
        size = sum(p[2] for p in pieces)
        slot = table[(T_FSLOT if kind == "f" else T_HSLOT) + head]
        at_frame = table[T_FRAME] + frame
        at_height = table[T_HEIGHT] + height
        reaches = True
        if frame:
            reaches = reaches & (reach[head, 0] > 0)
        if height:
            reaches = reaches & (reach[head, 1] > 0)
        here = base + jnp.where(reaches, slot, 0)

        @pl.when(reaches)
        def _(here=here):
            pltpu.make_async_copy(bufs[0].at[0], held.at[here], sem.at[here]).wait()

        inside = (at_frame >= 0) & (at_frame < lax.axis_size("tm"))
        inside = inside & (at_height >= 0) & (at_height < lax.axis_size("space")) & reaches
        for c in range(2):
            for w in range(2):
                g = w - c
                ok = inside & (mask[c, 9 * (frame + 1) + 3 * (height + 1) + g + 1] == 1)
                if g:
                    ok = ok & (reach[head, 2] > 0)
                lists[c, counts[c]] = here * 2 + w
                counts[c] = counts[c] + ok.astype(jnp.int32)
        base += size

    state = []
    for c in range(2):
        largest, total = get_stats(stat_in[0, c])
        acc_s[c] = acc_in[0, c]
        max_s[c] = jnp.broadcast_to(largest, (largest.shape[0], HD))
        sum_s[c] = jnp.broadcast_to(total, (total.shape[0], HD))

    spare = jnp.where(counts[0] > 0, lists[0, 0], lists[1, 0])

    def body(it, carry):
        for c in range(2):
            tiles = []
            for t in range(2):
                place = 2 * it + t
                valid = place < counts[c]
                entry = jnp.where(valid, lists[c, place], spare)
                slot, w = entry // 2, entry % 2
                tiles.append((held[slot, 0, w], held[slot, 1, w], valid))
            q = query[c]
            largest, total, acc = step(q, tiles, (max_s[c][:, 0:1], sum_s[c][:, 0:1], acc_s[c]))
            acc_s[c] = acc
            max_s[c] = jnp.broadcast_to(largest, (largest.shape[0], HD))
            sum_s[c] = jnp.broadcast_to(total, (total.shape[0], HD))
        return carry

    rounds = (jnp.maximum(counts[0], counts[1]) + 1) // 2
    lax.fori_loop(0, rounds, body, 0)
    for c in range(2):
        out[c] = (acc_s[c] / sum_s[c][:, 0:1]).astype(BF)
        if not last:
            acc_out[0, c] = acc_s[c]
            put_stats(stat_out, (0, c), max_s[c][:, 0:1], sum_s[c][:, 0:1])


def branch(most_h, most_c, most_f, queries, keys, values, mask, reach, table):
    nw, tile, width = queries.shape
    heads = width // HD
    unit = (2, nw, tile, HD)
    rest_h = most_h - most_c
    sizes = [(T_HORD, 0, most_c)]
    if rest_h:
        sizes.append((T_HORD, most_c, rest_h))
    sizes.append((T_FORD, 0, most_f))
    slots = most_h + most_f
    packed = pl.pallas_call(
        functools.partial(pack_kernel, sizes),
        name="pack",
        in_specs=[SMEM, ANY, ANY],
        out_specs=[ANY] * len(sizes),
        out_shape=[jax.ShapeDtypeStruct((n,) + unit, BF) for _, _, n in sizes],
        scratch_shapes=[
            pltpu.VMEM((slots,) + unit, BF),
            pltpu.SemaphoreType.DMA((slots, 2)),
            pltpu.SemaphoreType.DMA((slots,)),
        ],
        cost_estimate=pl.CostEstimate(flops=0, bytes_accessed=slots << 19, transcendentals=0),
    )(table, keys, values)
    first = packed[0]
    low1, high1 = shift(first, "space", 1), shift(first, "space", -1)
    frame_lo, frame_hi = shift(packed[-1], "tm", 1), shift(packed[-1], "tm", -1)
    corners = [shift(b, "tm", by) for by in (1, -1) for b in (low1, high1)]
    if rest_h:
        low2, high2 = shift(packed[1], "space", 1), shift(packed[1], "space", -1)

    block = pl.BlockSpec((nw, tile, HD), lambda i: (0, 0, i))
    state_block = pl.BlockSpec((1, nw, tile, HD), lambda i: (i, 0, 0, 0))
    state = jax.ShapeDtypeStruct((heads, nw, tile, HD), F32)
    acc, stats = pl.pallas_call(
        own_kernel,
        name="own",
        grid=(heads,),
        in_specs=[SMEM, SMEM, block, block, block],
        out_specs=[state_block, state_block],
        out_shape=[state, state],
        cost_estimate=pl.CostEstimate(
            flops=heads * 4 * 4 * tile * tile * HD, bytes_accessed=12 << 20, transcendentals=heads * 4 * tile * tile
        ),
    )(reach, mask, queries, keys, values)

    def far(spec, bufs, last, steps, slots, previous, acc, stats):
        order = lambda i, table, reach, mask: (0, 0, table[T_HORD + i])
        by_head = lambda i, table, reach, mask: (table[T_HORD + i], 0, 0, 0)
        by_slot = lambda i, table, reach, mask: (i, 0, 0, 0)
        data = pl.BlockSpec((nw, tile, HD), order)
        head_state = pl.BlockSpec((1, nw, tile, HD), by_slot if last else by_head)
        slot_state = pl.BlockSpec((1, nw, tile, HD), by_slot)
        in_specs = [ANY] * len(bufs) + ([ANY] if last else []) + [data, head_state, head_state]
        out_specs = [data] if last else [data, slot_state, slot_state]
        out_shape = [jax.ShapeDtypeStruct((nw, tile, width), BF)]
        if not last:
            out_shape += [state, state]
        args = list(bufs) + ([previous] if last else []) + [queries, acc, stats]
        entries = sum(len(s[3]) for s in spec)
        return pl.pallas_call(
            functools.partial(far_kernel, spec, last),
            name="corner" if last else "near",
            grid_spec=pltpu.PrefetchScalarGridSpec(
                num_scalar_prefetch=3,
                grid=(steps,),
                in_specs=in_specs,
                out_specs=out_specs,
                scratch_shapes=[
                    pltpu.VMEM((slots,) + unit, BF),
                    pltpu.SemaphoreType.DMA((slots,)),
                    pltpu.VMEM((nw, tile, HD), F32),
                    pltpu.VMEM((nw, tile, HD), F32),
                    pltpu.VMEM((nw, tile, HD), F32),
                    pltpu.SMEM((nw, 16), jnp.int32),
                ],
            ),
            out_shape=out_shape,
            input_output_aliases={3 + len(bufs): 0} if last else {},
            cost_estimate=pl.CostEstimate(
                flops=slots * 4 * tile * tile * HD * 4, bytes_accessed=slots << 18, transcendentals=slots * 4 * tile * tile
            ),
        )(table, reach, mask, *args)

    bufs, spec = [], []
    for height, parts in ((-1, [low1] + ([low2] if rest_h else [])), (1, [high1] + ([high2] if rest_h else []))):
        pieces, start = [], 0
        for part in parts:
            pieces.append((len(bufs), start, part.shape[0]))
            start += part.shape[0]
            bufs.append(part)
        spec.append((0, height, "h", pieces))
    for frame, part in ((-1, frame_lo), (1, frame_hi)):
        spec.append((frame, 0, "f", [(len(bufs), 0, most_f)]))
        bufs.append(part)
    out, acc, stats = far(spec, bufs, False, heads, 2 * (most_h + most_f), None, acc, stats)
    spec = [(f, e, "c", [(j, 0, most_c)]) for j, (f, e) in enumerate(((-1, -1), (-1, 1), (1, -1), (1, 1)))]
    (out,) = far(spec, corners, True, most_c, 4 * most_c, out, acc, stats)
    return out


def local(queries, keys, values, tile_mask, head_reach):
    queries, keys, values, mask = queries[0, 0], keys[0, 0], values[0, 0], tile_mask[0, 0]
    heads = queries.shape[2] // HD
    table = pl.pallas_call(
        functools.partial(meta_kernel, heads, BRANCHES),
        name="meta",
        in_specs=[SMEM],
        out_specs=SMEM,
        out_shape=jax.ShapeDtypeStruct((T_LEN,), jnp.int32),
    )(head_reach)
    run = [functools.partial(branch, *sizes) for sizes in BRANCHES]
    args = (queries, keys, values, mask, head_reach, table)
    if len(run) == 1:
        out = run[0](*args)
    else:
        out = lax.switch(table[T_PICK], run, *args)
    return out[None, None]


def solution(mesh):
    in_specs = (
        P("tm", "space", None, None, None),
        P("tm", "space", None, None, None),
        P("tm", "space", None, None, None),
        P("tm", "space", None, None),
        P(),
    )
    out_specs = P("tm", "space", None, None, None)
    return jax.shard_map(local, mesh=mesh, in_specs=in_specs, out_specs=out_specs, check_vma=False)
```

time: 587 us -> 216 us (0.37)
  matrix products: 135 us -> 0 us
  waiting for transfers between devices: 217 us -> 105 us
  Pallas kernels: 0 us -> 80.7 us
  local copies, waits for them, and re-layouts: 78.2 us -> 1.36 us
  other arithmetic: 70.2 us -> 0 us
  loops' own time: 59 us -> 0 us
    dot_general x48 -> x0, matrix products: 135 us -> none  [the longest x24 68.1 us: per_head(): jnp.dot(rounded, value_head, preferred_element_type=jnp.float32) / totals]
    ppermute x4 -> x8, waiting for transfers between devices: 217 us -> 105 us  [shift(): lax.ppermute(value, axis, [(i, i + by) for i in range(count) if 0 <= i +...]
    pallas_call x0 -> x5, Pallas kernels: none -> 80.7 us  [the longest x2 58.6 us: far(): pl.pallas_call(functools.partial(far_kernel, spec, last), name='corner' i...]
    another operation x2 -> x0, loops' own time: 59 us -> none  [attend(): result = lax.map(per_head, jnp.arange(heads, dtype=jnp.int32))]
    slice x2 -> x0, local copies, waits for them, and re-layouts: 53.6 us -> none  [the longest x1 53.6 us: local(): value_rows = padded[1, :, :, column:column + 3].reshape(-1, width)]
    reduce_sum x24 -> x0, other arithmetic: 36.5 us -> none  [per_head(): totals = jnp.sum(weights, axis=1, keepdims=True)]
    concatenate x2 -> x0, other arithmetic: 30.8 us -> none  [the longest x1 26.3 us: plane_step_in(): return jnp.concatenate([above, block, below], axis=2)]
    dynamic_slice x48 -> x0, local copies, waits for them, and re-layouts: 16.5 us -> none  [the longest x24 14 us: attend(): result = lax.map(per_head, jnp.arange(heads, dtype=jnp.int32))]
  transfers between devices with their start and end apart: 4 -> 8, of which waited for: 3 -> 3; matrix products, arithmetic and copies ran while one was open for 1% -> 0% of each run, Pallas kernels for 0% -> 22%
where the time goes in v1:
time: 216 us
  waiting for transfers between devices  105 us (49%)
  Pallas kernels  80.7 us (37%)
  starting transfers between devices  28.5 us (13%)
    ppermute x8, waiting for transfers between devices, shift(): lax.ppermute(value, axis, [(i, i + by) for i in range(count) if 0 <= i +...  105 us
    pallas_call x2, Pallas kernels, far(): pl.pallas_call(functools.partial(far_kernel, spec, last), name='corner' i...  58.6 us
    ppermute x8, starting transfers between devices, shift(): lax.ppermute(value, axis, [(i, i + by) for i in range(count) if 0 <= i +...  28.5 us
    pallas_call x1, Pallas kernels, branch(): pl.pallas_call(own_kernel, name='own', grid=(heads,), in_specs=[SMEM, SME...  13.8 us
    pallas_call x1, Pallas kernels, branch(): pl.pallas_call(functools.partial(pack_kernel, sizes), name='pack', in_spe...  6.63 us
  transfers between devices with their start and end apart: 8, of which 3 were waited for; matrix products, arithmetic and copies ran while one was open for 0% of the time, Pallas kernels for 22%

profile of v1, /device:TPU:6, one launch (start us, length us, event | category | flops | bytes accessed | tf_op | source)
XLA Modules:
  0.0 216.1 jit_solution(433022965440810156)
XLA Ops:
  0.0 1.4 copy.7.reach
  1.4 1.7 meta.1.table
  3.0 6.6 %pack.1 = (bf16[12,2,2,256,128]{4,3,2,1,0:T(8,128)(2,1)}, bf16[12,2,2,256,128]{4,3,2,1,0:T(8,128)(2,1)}) custom-call(s32[80]{0:T(128)} %meta.1.table, bf16[2,256,1536]{2,1,0:T(8,128)(2,1)} %bitcast.5, bf16[2,256,1536]{2,1,0:T(8,128)(2,1)} %bitcast.7), custom_call_target="tpu_custom_call" | custom-call | bytes 12582912 | tf_op jit(solution)/shard_map/pack/pallas_call | solution.py:248
  9.7 3.5 %collective-permute-start = (bf16[12,2,2,256,128]{4,3,2,1,0:T(8,128)(2,1)}, bf16[12,2,2,256,128]{4,3,2,1,0:T(8,128)(2,1)S(1)}, u32[]{:S(2)}, u32[]{:S(2)}) collective-permute-start(bf16[12,2,2,256,128]{4,3,2,1,0:T(8,128)(2,1)} %get-tuple-element.12), channel_id=1, source_target_pairs={{0,1},{1,2},{2,3},{3,4},{4,5},{5,6},{6,7},{7,8},{8,9},{9,10},{10,1... | collective-permute-start | bytes 9437192 | tf_op jit(solution)/shard_map/ppermute | solution.py:29
  13.2 7.1 %collective-permute-start.2 = (bf16[12,2,2,256,128]{4,3,2,1,0:T(8,128)(2,1)}, bf16[12,2,2,256,128]{4,3,2,1,0:T(8,128)(2,1)}, u32[]{:S(2)}, u32[]{:S(2)}) collective-permute-start(bf16[12,2,2,256,128]{4,3,2,1,0:T(8,128)(2,1)} %get-tuple-element.12), channel_id=1, source_target_pairs={{1,0},{2,1},{3,2},{4,3},{5,4},{6,5},{7,6},{8,7},{9,8},{10,9},{11,1... | collective-permute-start | bytes 9437192 | tf_op jit(solution)/shard_map/ppermute | solution.py:29
  20.3 1.9 collective-permute-start.6
  22.2 5.1 %collective-permute-start.7 = (bf16[12,2,2,256,128]{4,3,2,1,0:T(8,128)(2,1)}, bf16[12,2,2,256,128]{4,3,2,1,0:T(8,128)(2,1)}, u32[]{:S(2)}, u32[]{:S(2)}) collective-permute-start(bf16[12,2,2,256,128]{4,3,2,1,0:T(8,128)(2,1)} %get-tuple-element.13), channel_id=1, source_target_pairs={{32,0},{64,32},{96,64},{33,1},{65,33},{97,65},{34,2},{66,34},{98,6... | collective-permute-start | bytes 9437192 | tf_op jit(solution)/shard_map/ppermute | solution.py:29
  27.3 59.3 %collective-permute-done.rest_0_ = bf16[12,2,2,256,128]{4,3,2,1,0:T(8,128)(2,1)S(1)} collective-permute-done((bf16[12,2,2,256,128]{4,3,2,1,0:T(8,128)(2,1)}, bf16[12,2,2,256,128]{4,3,2,1,0:T(8,128)(2,1)S(1)}, u32[]{:S(2)}, u32[]{:S(2)}) %collective-permute-start) | collective-permute-done | bytes 3145760 | tf_op jit(solution)/shard_map/ppermute | solution.py:29
  86.6 0.0 copy-start
  86.6 1.9 collective-permute-start.1
  88.5 5.1 %collective-permute-start.4 = (bf16[12,2,2,256,128]{4,3,2,1,0:T(8,128)(2,1)S(1)}, bf16[12,2,2,256,128]{4,3,2,1,0:T(8,128)(2,1)}, u32[]{:S(2)}, u32[]{:S(2)}) collective-permute-start(bf16[12,2,2,256,128]{4,3,2,1,0:T(8,128)(2,1)S(1)} %collective-permute-done.rest_0_), channel_id=1, source_target_pairs={{32,0},{64,32},{96,64},{33,1},{65,33},{97,65},{34,2},{66,34},{98,6... | collective-permute-start | bytes 9437192 | tf_op jit(solution)/shard_map/ppermute | solution.py:29
  93.7 0.0 collective-permute-done.2.rest_1_
  93.7 1.9 collective-permute-start.3
  95.6 27.5 %collective-permute-done.6.rest_2_ = bf16[12,2,2,256,128]{4,3,2,1,0:T(8,128)(2,1)} collective-permute-done((bf16[12,2,2,256,128]{4,3,2,1,0:T(8,128)(2,1)}, bf16[12,2,2,256,128]{4,3,2,1,0:T(8,128)(2,1)}, u32[]{:S(2)}, u32[]{:S(2)}) %collective-permute-start.6) | collective-permute-done | bytes 3145760 | tf_op jit(solution)/shard_map/ppermute | solution.py:29
  123.2 1.9 collective-permute-start.5
  125.1 13.8 %own.1 = (f32[12,2,256,128]{3,2,1,0:T(8,128)}, f32[12,2,256,128]{3,2,1,0:T(8,128)}) custom-call(s32[12,3]{1,0:T(8,128)} %copy.7.reach, s32[2,27]{1,0:T(2,128)} %bitcast.12, bf16[2,256,1536]{2,1,0:T(8,128)(2,1)} %bitcast.9, bf16[2,256,1536]{2,1,0:T(8,128)(2,1)} %bitcast.6, bf16[2,256,1536]{2,1,0:T(8,128)(2,1)} %bitcast.8), custom_call_target="tpu_custom_call" | custom-call | flops 1610612736 | bytes 12582912 | tf_op jit(solution)/shard_map/own/pallas_call | solution.py:271
  138.9 0.0 collective-permute-done.7.rest_3_
  138.9 0.0 copy-done
  138.9 33.1 %near.1 = (bf16[2,256,1536]{2,1,0:T(8,128)(2,1)}, f32[12,2,256,128]{3,2,1,0:T(8,128)}, f32[12,2,256,128]{3,2,1,0:T(8,128)}) custom-call(s32[80]{0:T(128)} %meta.1.table, s32[12,3]{1,0:T(8,128)} %copy.7.reach, s32[2,27]{1,0:T(2,128)} %bitcast.13, bf16[12,2,2,256,128]{4,3,2,1,0:T(8,128)(2,1)} %copy-done, ...), custom_call_target="tpu_custom_call" | custom-call | flops 6442450944 | bytes 12582912 | tf_op jit(solution)/shard_map/near/pallas_call | solution.py:297
  172.0 0.0 collective-permute-done.1.rest_0_
  172.0 18.6 %collective-permute-done.3.rest_1_ = bf16[12,2,2,256,128]{4,3,2,1,0:T(8,128)(2,1)} collective-permute-done((bf16[12,2,2,256,128]{4,3,2,1,0:T(8,128)(2,1)}, bf16[12,2,2,256,128]{4,3,2,1,0:T(8,128)(2,1)}, u32[]{:S(2)}, u32[]{:S(2)}) %collective-permute-start.3) | collective-permute-done | bytes 3145760 | tf_op jit(solution)/shard_map/ppermute | solution.py:29
  190.6 0.0 collective-permute-done.4.rest_2_
  190.6 0.0 collective-permute-done.5.rest_3_
  190.6 25.5 %corner.1 = bf16[2,256,1536]{2,1,0:T(8,128)(2,1)} custom-call(s32[80]{0:T(128)} %meta.1.table, s32[12,3]{1,0:T(8,128)} %copy.7.reach, s32[2,27]{1,0:T(2,128)} %bitcast.14, bf16[12,2,2,256,128]{4,3,2,1,0:T(8,128)(2,1)} %collective-permute-done.1.rest_0_, bf16[12,2,2,256,128]{4,3,2,1,0:T(8,128)(2,1)} %collective-permute-done.3.rest_1_, ...), custom_call_target="tpu_custom_call", output_to_operand_aliasing={{}: (7, {})} | custom-call | flops 6442450944 | bytes 12582912 | tf_op jit(solution)/shard_map/corner/pallas_call | solution.py:297
Async XLA Ops:
  9.7 77.0 %collective-permute-start = (bf16[12,2,2,256,128]{4,3,2,1,0:T(8,128)(2,1)}, bf16[12,2,2,256,128]{4,3,2,1,0:T(8,128)(2,1)S(1)}, u32[]{:S(2)}, u32[]{:S(2)}) collective-permute-start(bf16[12,2,2,256,128]{4,3,2,1,0:T(8,128)(2,1)} %get-tuple-element.12), channel_id=1, source_target_pairs={{0,1},{1,2},{2,3},{3,4},{4,5},{5,6},{6,7},{7,8},{8,9},{9,10},{10,1... | collective-permute-start | bytes 9437192 | tf_op jit(solution)/shard_map/ppermute | solution.py:29
  13.2 80.5 %collective-permute-start.2 = (bf16[12,2,2,256,128]{4,3,2,1,0:T(8,128)(2,1)}, bf16[12,2,2,256,128]{4,3,2,1,0:T(8,128)(2,1)}, u32[]{:S(2)}, u32[]{:S(2)}) collective-permute-start(bf16[12,2,2,256,128]{4,3,2,1,0:T(8,128)(2,1)} %get-tuple-element.12), channel_id=1, source_target_pairs={{1,0},{2,1},{3,2},{4,3},{5,4},{6,5},{7,6},{8,7},{9,8},{10,9},{11,1... | collective-permute-start | bytes 9437192 | tf_op jit(solution)/shard_map/ppermute | solution.py:29
  20.3 102.9 %collective-permute-start.6 = (bf16[12,2,2,256,128]{4,3,2,1,0:T(8,128)(2,1)}, bf16[12,2,2,256,128]{4,3,2,1,0:T(8,128)(2,1)}, u32[]{:S(2)}, u32[]{:S(2)}) collective-permute-start(bf16[12,2,2,256,128]{4,3,2,1,0:T(8,128)(2,1)} %get-tuple-element.13), channel_id=1, source_target_pairs={{0,32},{32,64},{64,96},{1,33},{33,65},{65,97},{2,34},{34,66},{66,9... | collective-permute-start | bytes 9437192 | tf_op jit(solution)/shard_map/ppermute | solution.py:29
  22.2 116.7 %collective-permute-start.7 = (bf16[12,2,2,256,128]{4,3,2,1,0:T(8,128)(2,1)}, bf16[12,2,2,256,128]{4,3,2,1,0:T(8,128)(2,1)}, u32[]{:S(2)}, u32[]{:S(2)}) collective-permute-start(bf16[12,2,2,256,128]{4,3,2,1,0:T(8,128)(2,1)} %get-tuple-element.13), channel_id=1, source_target_pairs={{32,0},{64,32},{96,64},{33,1},{65,33},{97,65},{34,2},{66,34},{98,6... | collective-permute-start | bytes 9437192 | tf_op jit(solution)/shard_map/ppermute | solution.py:29
  86.6 52.3 %copy-start = (bf16[12,2,2,256,128]{4,3,2,1,0:T(8,128)(2,1)}, bf16[12,2,2,256,128]{4,3,2,1,0:T(8,128)(2,1)S(1)}, u32[]{:S(2)}) copy-start(bf16[12,2,2,256,128]{4,3,2,1,0:T(8,128)(2,1)S(1)} %collective-permute-done.rest_0_) | copy-start | bytes 9437188
  86.6 85.4 %collective-permute-start.1 = (bf16[12,2,2,256,128]{4,3,2,1,0:T(8,128)(2,1)S(1)}, bf16[12,2,2,256,128]{4,3,2,1,0:T(8,128)(2,1)}, u32[]{:S(2)}, u32[]{:S(2)}) collective-permute-start(bf16[12,2,2,256,128]{4,3,2,1,0:T(8,128)(2,1)S(1)} %collective-permute-done.rest_0_), channel_id=1, source_target_pairs={{0,32},{32,64},{64,96},{1,33},{33,65},{65,97},{2,34},{34,66},{66,9... | collective-permute-start | bytes 9437192 | tf_op jit(solution)/shard_map/ppermute | solution.py:29
  88.5 102.1 %collective-permute-start.4 = (bf16[12,2,2,256,128]{4,3,2,1,0:T(8,128)(2,1)S(1)}, bf16[12,2,2,256,128]{4,3,2,1,0:T(8,128)(2,1)}, u32[]{:S(2)}, u32[]{:S(2)}) collective-permute-start(bf16[12,2,2,256,128]{4,3,2,1,0:T(8,128)(2,1)S(1)} %collective-permute-done.rest_0_), channel_id=1, source_target_pairs={{32,0},{64,32},{96,64},{33,1},{65,33},{97,65},{34,2},{66,34},{98,6... | collective-permute-start | bytes 9437192 | tf_op jit(solution)/shard_map/ppermute | solution.py:29
  93.7 96.9 %collective-permute-start.3 = (bf16[12,2,2,256,128]{4,3,2,1,0:T(8,128)(2,1)}, bf16[12,2,2,256,128]{4,3,2,1,0:T(8,128)(2,1)}, u32[]{:S(2)}, u32[]{:S(2)}) collective-permute-start(bf16[12,2,2,256,128]{4,3,2,1,0:T(8,128)(2,1)} %collective-permute-done.2.rest_1_), channel_id=1, source_target_pairs={{0,32},{32,64},{64,96},{1,33},{33,65},{65,97},{2,34},{34,66},{66,9... | collective-permute-start | bytes 9437192 | tf_op jit(solution)/shard_map/ppermute | solution.py:29
  123.2 67.4 %collective-permute-start.5 = (bf16[12,2,2,256,128]{4,3,2,1,0:T(8,128)(2,1)}, bf16[12,2,2,256,128]{4,3,2,1,0:T(8,128)(2,1)}, u32[]{:S(2)}, u32[]{:S(2)}) collective-permute-start(bf16[12,2,2,256,128]{4,3,2,1,0:T(8,128)(2,1)} %collective-permute-done.2.rest_1_), channel_id=1, source_target_pairs={{32,0},{64,32},{96,64},{33,1},{65,33},{97,65},{34,2},{66,34},{98,6... | collective-permute-start | bytes 9437192 | tf_op jit(solution)/shard_map/ppermute | solution.py:29
